TPU v7x, 32 devices: a whole 2x2x4 slice. The times are simulated.
32 devices in a mesh: section: 2 (over x), mirror: 2 (over y), dp: 8 (over z, core).
Axes of the slice: x: 2, y: 2, z: 4, core: 2. Of those that a mesh axis runs over, the one named last changes fastest.
Arguments:
- sent_fwd: bfloat16 [2, 2, 8, 4096], P('section', 'mirror', 'dp'), may hold values from -36 to 36
- sent_bwd: bfloat16 [2, 2, 8, 4096], P('section', 'mirror', 'dp'), may hold values from -6 to 6
- stash: bfloat16 [2, 2, 8, 4096], P('section', 'mirror', 'dp'), may hold values from -36 to 36
- gain: float32 [2, 4096], P('section'), may hold values from 0.5 to 1.5
- w_in: bfloat16 [2, 4096, 1024], P('section', None, 'dp'), may hold values from -0.09375 to 0.09375
- w_out: bfloat16 [2, 1024, 4096], P('section', 'dp'), may hold values from -0.375 to 0.375
Outputs:
- fwd_out: bfloat16 [2, 2, 8, 4096], P('section', 'mirror', 'dp')
- bwd_out: bfloat16 [2, 2, 8, 4096], P('section', 'mirror', 'dp')
- w_in_grad: bfloat16 [2, 4096, 1024], P('section', 'mirror', 'dp')
- w_out_grad: bfloat16 [2, 1024, 4096], P('section', 'dp', 'mirror')
All inputs are finite; a program needn't handle non-finite values.
Results may differ from a plain program's by a relative error of at most 0.0068.
Values may be sent and summed in bfloat16 or wider, within the bound.
No kernel may reach another device: no remote copies, remote signals or barrier semaphores. Data moves between devices by JAX's collectives and lax.ppermute only.
A program may use at most 64 MiB of HBM per device.

v0:
```python
import jax
import jax.numpy as jnp
from jax import lax
from jax.sharding import PartitionSpec as P


def extended_2(block, sides, width):
    for axis, dim in sides:
        count = lax.axis_size(axis)
        forward = [(i, i + 1) for i in range(count - 1)]
        forward.append((count - 1, 0))
        backward = [(target, source) for source, target in forward]
        low = lax.ppermute(
            lax.slice_in_dim(block, block.shape[dim] - width, None, axis=dim), axis, forward
        )
        high = lax.ppermute(lax.slice_in_dim(block, 0, width, axis=dim), axis, backward)
        block = jnp.concatenate([low, block, high], axis=dim)
    return block


def swapped(value, axis, apart):
    mask = 2**apart
    pairs = [(source, source ^ mask) for source in range(lax.axis_size(axis))]
    return lax.ppermute(value, axis, pairs)


def norm_rows(x):
    centre = x - jnp.mean(x, axis=-1, keepdims=True)
    rstd = lax.rsqrt(jnp.mean(centre * centre, axis=-1, keepdims=True) + 1e-05)
    return (centre * rstd, rstd)


def gelu_pair(h):
    coeff = 0.7978845608028654
    inner = coeff * (h + 0.044715 * h * h * h)
    tanh_val = jnp.tanh(inner)
    value = 0.5 * h * (1.0 + tanh_val)
    slope = 0.5 * (1.0 + tanh_val) + 0.5 * h * (1.0 - tanh_val * tanh_val) * coeff * (
        1.0 + 3.0 * 0.044715 * h * h
    )
    return (value, slope)


def rounded(values):
    return lax.optimization_barrier(values.astype(jnp.bfloat16)).astype(jnp.float32)


def on_device(sent_fwd, sent_bwd, stash, gain, w_in, w_out):
    mirror_pos = lax.axis_index("mirror")
    downward = mirror_pos == 0
    fwd_local = sent_fwd[0, 0]
    bwd_local = sent_bwd[0, 0]
    upward_load = jnp.where(downward, fwd_local, bwd_local)
    lower_load = jnp.where(downward, bwd_local, fwd_local)
    block = jnp.stack([lower_load, upward_load])
    extended = extended_2(block, (("section", 0),), 1)
    from_lower = extended[0]
    from_upper = extended[3]
    fwd_in = jnp.where(downward, from_lower, from_upper)
    bwd_in = jnp.where(downward, from_upper, from_lower)
    gain_row = gain[0]
    w_first = w_in[0]
    w_second = w_out[0]
    x_fwd = fwd_in.astype(jnp.float32)
    nhat_fwd, _ = norm_rows(x_fwd)
    normed_fwd = (nhat_fwd * gain_row).astype(jnp.bfloat16)
    nhat_bwd, rstd_bwd = norm_rows(stash[0, 0].astype(jnp.float32))
    normed_bwd = (nhat_bwd * gain_row).astype(jnp.bfloat16)
    whole_fwd, whole_bwd, whole_cotan = (
        lax.all_gather(normed_fwd, "dp", axis=0, tiled=True),
        lax.all_gather(normed_bwd, "dp", axis=0, tiled=True),
        lax.all_gather(bwd_in, "dp", axis=0, tiled=True),
    )
    hidden_fwd = jnp.dot(whole_fwd, w_first, preferred_element_type=jnp.float32)
    acted_fwd = gelu_pair(hidden_fwd)[0].astype(jnp.bfloat16)
    hidden_bwd = jnp.dot(whole_bwd, w_first, preferred_element_type=jnp.float32)
    value_bwd, slope_bwd = gelu_pair(hidden_bwd)
    acted_bwd = value_bwd.astype(jnp.bfloat16)
    d_acted = jnp.dot(whole_cotan, w_second.T, preferred_element_type=jnp.float32)
    d_hidden = (d_acted * slope_bwd).astype(jnp.bfloat16)
    piece = acted_fwd
    branch_sum = lax.psum_scatter(
        jnp.dot(piece, w_second, preferred_element_type=jnp.float32),
        "dp",
        scatter_dimension=0,
        tiled=True,
    )
    piece = d_hidden
    d_normed = lax.psum_scatter(
        jnp.dot(piece, w_first.T, preferred_element_type=jnp.float32),
        "dp",
        scatter_dimension=0,
        tiled=True,
    )
    fwd_result = (x_fwd + branch_sum).astype(jnp.bfloat16)
    scaled = d_normed * gain_row
    d_input = rstd_bwd * (
        scaled
        - jnp.mean(scaled, axis=-1, keepdims=True)
        - nhat_bwd * jnp.mean(scaled * nhat_bwd, axis=-1, keepdims=True)
    )
    bwd_result = (bwd_in.astype(jnp.float32) + d_input).astype(jnp.bfloat16)
    half_width = w_first.shape[0] // 2
    own_start = mirror_pos * half_width
    other_start = (1 - mirror_pos) * half_width
    grad_first = rounded(jnp.dot(whole_bwd.T, d_hidden, preferred_element_type=jnp.float32))
    summed_first = lax.psum_scatter(
        grad_first.astype(jnp.bfloat16), "mirror", scatter_dimension=0, tiled=True
    )
    outgoing = (acted_bwd, lax.dynamic_slice_in_dim(whole_cotan, other_start, half_width, 1))
    far_acted, far_cotan = swapped((outgoing[0], outgoing[1]), "mirror", 0)
    own_second = jnp.dot(
        acted_bwd.T,
        lax.dynamic_slice_in_dim(whole_cotan, own_start, half_width, 1),
        preferred_element_type=jnp.float32,
    )
    far_second = jnp.dot(far_acted.T, far_cotan, preferred_element_type=jnp.float32)
    summed_second = rounded(own_second) + rounded(far_second)
    return (
        fwd_result[None, None],
        bwd_result[None, None],
        summed_first[None],
        summed_second.astype(jnp.bfloat16)[None],
    )


def solution(mesh):
    in_specs = (
        P("section", "mirror", "dp", None),
        P("section", "mirror", "dp", None),
        P("section", "mirror", "dp", None),
        P("section", None),
        P("section", None, "dp"),
        P("section", "dp", None),
    )
    out_specs = (
        P("section", "mirror", "dp", None),
        P("section", "mirror", "dp", None),
        P("section", "mirror", "dp"),
        P("section", "dp", "mirror"),
    )
    return jax.shard_map(
        on_device, mesh=mesh, in_specs=in_specs, out_specs=out_specs, check_vma=False
    )
```

profile of v0, /device:TPU:0, one launch (start us, length us, event | category | flops | bytes accessed | tf_op | source)
XLA Modules:
  0.0 135.8 jit_solution(11940512752795791094)
XLA Ops:
  8.1 0.9 fusion.21
  9.0 3.0 %collective-permute-start.1 = (bf16[1,1,4096]{2,1,0:T(2,128)(2,1)S(1)}, bf16[1,1,4096]{2,1,0:T(2,128)(2,1)S(1)}, u32[]{:S(2)}, u32[]{:S(2)}) collective-permute-start(bf16[1,1,4096]{2,1,0:T(2,128)(2,1)S(1)} %get-tuple-element.13), channel_id=1, source_target_pairs={{16,0},{0,16},{17,1},{1,17},{18,2},{2,18},{19,3},{3,19},{20,4},{4,... | collective-permute-start | bytes 24584 | tf_op jit(solution)/shard_map/ppermute | solution.py:16
  12.1 1.4 convert_reduce_fusion
  14.1 1.4 %multiply_reduce_fusion = f32[]{:T(128)} fusion(bf16[1,1,1,4096]{3,2,1,0:T(2,128)(2,1)} %param.8, f32[]{:T(128)S(6)} %div.20), kind=kLoop, calls=%fused_computation.49 | loop fusion | flops 16383 | bytes 8200 | tf_op jit(solution)/shard_map/reduce_sum | solution.py:29
  16.1 1.3 dynamic-slice.2
  17.4 0.6 fusion.59
  18.7 0.6 multiply_reduce_fusion.1
  20.0 0.8 fusion.27
  20.8 14.7 %all-gather.1 = bf16[8,1,4096]{2,1,0:T(2,128)(2,1)S(1)} all-gather(bf16[1,1,4096]{2,1,0:T(2,128)(2,1)S(1)} %get-tuple-element.16), channel_id=1, replica_groups=mesh['section'=2,'mirror'=2,'dp'=8] {'dp'}, dimensions={0}, use_global_device_ids=true | all-gather | bytes 73728 | tf_op jit(solution)/shard_map/all_gather | solution.py:70
  35.6 14.0 %all-gather = bf16[8,1,4096]{2,1,0:T(2,128)(2,1)S(1)} all-gather(bf16[1,1,4096]{2,1,0:T(2,128)(2,1)S(1)} %broadcast_select_fusion.2), channel_id=2, replica_groups=mesh['section'=2,'mirror'=2,'dp'=8] {'dp'}, dimensions={0}, use_global_device_ids=true | all-gather | bytes 73728 | tf_op jit(solution)/shard_map/all_gather | solution.py:72
  49.5 14.0 %all-gather.2 = bf16[8,1,4096]{2,1,0:T(2,128)(2,1)S(1)} all-gather(bf16[1,1,4096]{2,1,0:T(2,128)(2,1)S(1)} %get-tuple-element.15), channel_id=1, replica_groups=mesh['section'=2,'mirror'=2,'dp'=8] {'dp'}, dimensions={0}, use_global_device_ids=true | all-gather | bytes 73728 | tf_op jit(solution)/shard_map/all_gather | solution.py:71
  63.8 1.2 fusion.2
  65.0 0.4 fusion
  65.4 1.0 fusion.4
  66.5 1.5 %convolution_convert_fusion = bf16[4096,128]{1,0:T(8,128)(2,1)} fusion(bf16[8,128]{1,0:T(8,128)(2,1)S(1)} %fusion, bf16[8,1,4096]{2,1,0:T(2,128)(2,1)S(1)} %all-gather.2), kind=kOutput, calls=%fused_computation | convolution fusion | flops 8912896 | bytes 1116160 | tf_op jit(solution)/shard_map/dot_general | solution.py:106
  68.0 1.5 %collective-permute-start.2 = (bf16[8,128]{1,0:T(8,128)(2,1)S(1)}, bf16[8,128]{1,0:T(8,128)(2,1)S(1)}, u32[]{:S(2)}, u32[]{:S(2)}) collective-permute-start(bf16[8,128]{1,0:T(8,128)(2,1)S(1)} %get-tuple-element.17), channel_id=1, source_target_pairs={{0,8},{8,0},{1,9},{9,1},{2,10},{10,2},{3,11},{11,3},{4,12},{12,4},... | collective-permute-start | bytes 6152 | tf_op jit(solution)/shard_map/ppermute | solution.py:24
  69.8 0.6 collective-permute-start.3
  70.7 0.9 collective-permute-done.2
  71.6 2.1 %collective-permute-done.3 = bf16[8,2048]{1,0:T(8,128)(2,1)S(1)} collective-permute-done((bf16[8,2048]{1,0:T(8,128)(2,1)S(1)}, bf16[8,2048]{1,0:T(8,128)(2,1)S(1)}, u32[]{:S(2)}, u32[]{:S(2)}) %collective-permute-start.3) | collective-permute-done | bytes 32800 | tf_op jit(solution)/shard_map/ppermute | solution.py:24
  73.7 0.3 convolution_convert_fusion.1
  74.1 0.9 fusion.10
  75.0 47.7 %all-reduce.5.cloned.1.call-done = (f32[8,4096]{1,0:T(8,128)}, f32[8,4096]{1,0:T(8,128)}) async-done(((f32[8,4096]{1,0:T(8,128)}, f32[8,4096]{1,0:T(8,128)}), (f32[8,4096]{1,0:T(8,128)}, f32[8,4096]{1,0:T(8,128)})) %all-reduce.5.cloned.1.call-update) | async-done | bytes 262160
  122.7 2.2 %fusion.58 = (f32[]{:T(128)}, f32[]{:T(128)}, f32[1,4096]{1,0:T(1,128)S(1)}) fusion(f32[]{:T(128)S(6)} %rsqrt.9, f32[]{:T(128)S(6)} %div.20, bf16[1,1,1,4096]{3,2,1,0:T(2,128)(2,1)S(1)} %copy-done.2, f32[1,4096]{1,0:T(1,128)S(1)} %copy-done.3, f32[8,4096]{1,0:T(8,128)} %get-tuple-element.7, u32[]{:T(128)} %bitcast.15), kind=kLoop, calls=%fused_computation.79 | loop fusion | flops 28670 | bytes 57364 | tf_op jit(solution)/shard_map/reduce_sum | solution.py:99
  126.2 2.2 %fusion.23 = (bf16[1,1,1,4096]{3,2,1,0:T(2,128)(2,1)}, bf16[1,1,1,4096]{3,2,1,0:T(2,128)(2,1)}) fusion(bf16[1,1,4096]{2,1,0:T(2,128)(2,1)S(1)} %broadcast_select_fusion.2, f32[1,4096]{1,0:T(1,128)S(1)} %get-tuple-element.8, f32[]{:T(128)S(6)} %div.23, f32[]{:T(128)S(6)} %div.22, f32[]{:T(128)S(6)} %rsqrt.9, f32[]{:T(128)S(6)} %div.20, ...), kind=kLoop, calls=%fused_computation.35 | loop fusion | flops 49152 | bytes 84484 | tf_op jit(solution)/shard_map/broadcast_in_dim | solution.py:121
  (21 shorter events, 1.1 us)
Async XLA Ops:
  8.0 55.5 %copy-start = (bf16[1,4096,128]{2,1,0:T(8,128)(2,1)S(1)}, bf16[1,4096,128]{2,1,0:T(8,128)(2,1)}, u32[]{:S(2)}) copy-start(bf16[1,4096,128]{2,1,0:T(8,128)(2,1)} %param.10) | copy-start | bytes 3145732
  8.0 55.8 %copy-start.1 = (bf16[1,128,4096]{2,1,0:T(8,128)(2,1)S(1)}, bf16[1,128,4096]{2,1,0:T(8,128)(2,1)}, u32[]{:S(2)}) copy-start(bf16[1,128,4096]{2,1,0:T(8,128)(2,1)} %param.11) | copy-start | bytes 3145732
  8.0 114.7 %all-reduce.5.cloned.1.call-start = ((), (), s32[]{:S(2)}) async-start(), calls=%async_computation.2 | async-start | bytes 524288
  9.0 8.4 %collective-permute-start.1 = (bf16[1,1,4096]{2,1,0:T(2,128)(2,1)S(1)}, bf16[1,1,4096]{2,1,0:T(2,128)(2,1)S(1)}, u32[]{:S(2)}, u32[]{:S(2)}) collective-permute-start(bf16[1,1,4096]{2,1,0:T(2,128)(2,1)S(1)} %get-tuple-element.13), channel_id=1, source_target_pairs={{16,0},{0,16},{17,1},{1,17},{18,2},{2,18},{19,3},{3,19},{20,4},{4,... | collective-permute-start | bytes 24584 | tf_op jit(solution)/shard_map/ppermute | solution.py:16
  12.0 5.4 %collective-permute-start = (bf16[1,1,4096]{2,1,0:T(2,128)(2,1)S(1)}, bf16[1,1,4096]{2,1,0:T(2,128)(2,1)S(1)}, u32[]{:S(2)}, u32[]{:S(2)}) collective-permute-start(bf16[1,1,4096]{2,1,0:T(2,128)(2,1)S(1)} %get-tuple-element.14), channel_id=1, source_target_pairs={{0,16},{16,0},{1,17},{17,1},{2,18},{18,2},{3,19},{19,3},{4,20},{20... | collective-permute-start | bytes 24584 | tf_op jit(solution)/shard_map/ppermute | solution.py:13
  66.5 61.9 %reduce-scatter.2.cloned.1.call-start = ((), (), s32[]{:S(2)}) async-start(), calls=%async_computation.1 | async-start | bytes 1572864 | tf_op jit(solution)/shard_map/reduce_scatter | solution.py:107
  68.0 3.6 %collective-permute-start.2 = (bf16[8,128]{1,0:T(8,128)(2,1)S(1)}, bf16[8,128]{1,0:T(8,128)(2,1)S(1)}, u32[]{:S(2)}, u32[]{:S(2)}) collective-permute-start(bf16[8,128]{1,0:T(8,128)(2,1)S(1)} %get-tuple-element.17), channel_id=1, source_target_pairs={{0,8},{8,0},{1,9},{9,1},{2,10},{10,2},{3,11},{11,3},{4,12},{12,4},... | collective-permute-start | bytes 6152 | tf_op jit(solution)/shard_map/ppermute | solution.py:24
  69.8 4.0 %collective-permute-start.3 = (bf16[8,2048]{1,0:T(8,128)(2,1)S(1)}, bf16[8,2048]{1,0:T(8,128)(2,1)S(1)}, u32[]{:S(2)}, u32[]{:S(2)}) collective-permute-start(bf16[8,2048]{1,0:T(8,128)(2,1)S(1)} %bitcast.88), channel_id=1, source_target_pairs={{0,8},{8,0},{1,9},{9,1},{2,10},{10,2},{3,11},{11,3},{4,12},{12,4},... | collective-permute-start | bytes 98312 | tf_op jit(solution)/shard_map/ppermute | solution.py:24
  70.7 52.0 %copy-start.2 = (bf16[1,1,1,4096]{3,2,1,0:T(2,128)(2,1)S(1)}, bf16[1,1,1,4096]{3,2,1,0:T(2,128)(2,1)}, u32[]{:S(2)}) copy-start(bf16[1,1,1,4096]{3,2,1,0:T(2,128)(2,1)} %param.8) | copy-start | bytes 24580
  70.7 52.0 %copy-start.3 = (f32[1,4096]{1,0:T(1,128)S(1)}, f32[1,4096]{1,0:T(1,128)}, u32[]{:S(2)}) copy-start(f32[1,4096]{1,0:T(1,128)} %param.9) | copy-start | bytes 49156
Sparse Core Ops, SparseCore 0:
  66.6 56.0 all-reduce.4
Sparse Core Ops, SparseCore 1:
  69.8 21.2 reduce-scatter.1
where the time goes:
time: 136 us
  waiting for transfers between devices  50.7 us (37%)
  blocking collectives  42.7 us (31%)
  between operations  19.6 us (14%)
  other arithmetic  11 us (8%)
  starting transfers between devices  5.25 us (4%)
  matrix products  5.1 us (4%)
  local copies, waits for them, and re-layouts  1.47 us (1%)
    unnamed x3, waiting for transfers between devices  47.7 us
    all_gather x1, blocking collectives, on_device(): lax.all_gather(normed_fwd, 'dp', axis=0, tiled=True)  14.7 us
    all_gather x1, blocking collectives, on_device(): lax.all_gather(bwd_in, 'dp', axis=0, tiled=True)  14 us
    all_gather x1, blocking collectives, on_device(): lax.all_gather(normed_bwd, 'dp', axis=0, tiled=True)  14 us
    ppermute x2, waiting for transfers between devices, swapped(): return lax.ppermute(value, axis, pairs)  3.04 us
    ppermute x1, starting transfers between devices, extended_2(): lax.ppermute(lax.slice_in_dim(block, 0, width, axis=dim), axis, backward)  3 us
  transfers between devices with their start and end apart: 6, of which 3 were waited for; matrix products, arithmetic and copies ran while one was open for 9% of the time, Pallas kernels for 0%

commit v1 on v0

--- a/solution.py
+++ b/solution.py
@@ -2,6 +2,21 @@
 import jax.numpy as jnp
 from jax import lax
 from jax.sharding import PartitionSpec as P
+
+
+def chunk_watch(own_rows, peer_axis, array_axis):
+    all_rows = lax.axis_index(peer_axis)
+    carry_in = lax.axis_size(peer_axis)
+    seen_now, mid_arr, long_array = (carry_in, all_rows, own_rows.shape[array_axis])
+    spare, w2 = (own_rows, 1)
+    while w2 < seen_now:
+        even = range(seen_now)
+        current_value = map(lambda pp: (pp, (pp - w2) % seen_now), even)
+        passed = list(current_value)
+        carry = lax.ppermute(spare, peer_axis, passed)
+        spare = jnp.concatenate([spare, carry], axis=array_axis)
+        w2 = 2 * w2
+    return jnp.roll(spare, mid_arr * long_array, axis=array_axis)
 
 
 def extended_2(block, sides, width):
@@ -69,7 +84,7 @@
     whole_fwd, whole_bwd, whole_cotan = (
         lax.all_gather(normed_fwd, "dp", axis=0, tiled=True),
         lax.all_gather(normed_bwd, "dp", axis=0, tiled=True),
-        lax.all_gather(bwd_in, "dp", axis=0, tiled=True),
+        chunk_watch(bwd_in, "dp", 0),
     )
     hidden_fwd = jnp.dot(whole_fwd, w_first, preferred_element_type=jnp.float32)
     acted_fwd = gelu_pair(hidden_fwd)[0].astype(jnp.bfloat16)

time: 136 us -> 130 us (0.956)
  blocking collectives: 42.7 us -> 28.8 us
  starting transfers between devices: 5.25 us -> 9.33 us
  waiting for transfers between devices: 50.7 us -> 53.3 us
    all_gather x1 -> x0, blocking collectives: 14 us -> none  [on_device(): lax.all_gather(bwd_in, 'dp', axis=0, tiled=True)]
    ppermute x0 -> x3, waiting for transfers between devices: none -> 4.36 us  [chunk_watch(): carry = lax.ppermute(spare, peer_axis, passed)]
    ppermute x0 -> x3, starting transfers between devices: none -> 4.1 us  [chunk_watch(): carry = lax.ppermute(spare, peer_axis, passed)]
    ppermute x1, starting transfers between devices: 3 us -> 0.08 us  [extended_2(): lax.ppermute(lax.slice_in_dim(block, 0, width, axis=dim), axis, backward)]
    ppermute x1, starting transfers between devices: 0.08 us -> 3 us  [extended_2(): lax.ppermute(lax.slice_in_dim(block, block.shape[dim] - width, None, axis...]
    unnamed x3, waiting for transfers between devices: 47.7 us -> 45.9 us
  transfers between devices with their start and end apart: 6 -> 9, of which waited for: 3 -> 4; matrix products, arithmetic and copies ran while one was open for 9% -> 11% of each run, Pallas kernels for 0% -> 0%
where the time goes in v1:
time: 130 us; the launch traced here: 129 us
  waiting for transfers between devices  53.3 us (41%)
  blocking collectives  28.8 us (22%)
  between operations  19.6 us (15%)
  other arithmetic  11.1 us (9%)
  starting transfers between devices  9.33 us (7%)
  matrix products  6.33 us (5%)
    unnamed x3, waiting for transfers between devices  45.9 us
    all_gather x1, blocking collectives, on_device(): lax.all_gather(normed_fwd, 'dp', axis=0, tiled=True)  14.7 us
    all_gather x1, blocking collectives, on_device(): lax.all_gather(normed_bwd, 'dp', axis=0, tiled=True)  14.1 us
    ppermute x3, waiting for transfers between devices, chunk_watch(): carry = lax.ppermute(spare, peer_axis, passed)  4.36 us
    ppermute x3, starting transfers between devices, chunk_watch(): carry = lax.ppermute(spare, peer_axis, passed)  4.1 us
    ppermute x2, waiting for transfers between devices, swapped(): return lax.ppermute(value, axis, pairs)  3.02 us
    ppermute x1, starting transfers between devices, extended_2(): lax.ppermute(lax.slice_in_dim(block, block.shape[dim] - width, None, axis...  3 us
  transfers between devices with their start and end apart: 9, of which 4 were waited for; matrix products, arithmetic and copies ran while one was open for 11% of the time, Pallas kernels for 0%

profile of v1, /device:TPU:0, one launch (start us, length us, event | category | flops | bytes accessed | tf_op | source)
XLA Modules:
  0.0 129.4 jit_solution(7851458815520455005)
XLA Ops:
  8.1 0.9 fusion.22
  8.9 3.0 %collective-permute-start = (bf16[1,1,4096]{2,1,0:T(2,128)(2,1)S(1)}, bf16[1,1,4096]{2,1,0:T(2,128)(2,1)S(1)}, u32[]{:S(2)}, u32[]{:S(2)}) collective-permute-start(bf16[1,1,4096]{2,1,0:T(2,128)(2,1)S(1)} %get-tuple-element.12), channel_id=1, source_target_pairs={{0,16},{16,0},{1,17},{17,1},{2,18},{18,2},{3,19},{19,3},{4,20},{20... | collective-permute-start | bytes 24584 | tf_op jit(solution)/shard_map/ppermute | solution.py:28
  12.0 1.4 %convert_reduce_fusion = f32[]{:T(128)} fusion(bf16[1,1,1,4096]{3,2,1,0:T(2,128)(2,1)} %param.8), kind=kLoop, calls=%fused_computation.51 | loop fusion | flops 8191 | bytes 8196 | tf_op jit(solution)/shard_map/reduce_sum | solution.py:43
  14.0 1.4 %multiply_reduce_fusion = f32[]{:T(128)} fusion(bf16[1,1,1,4096]{3,2,1,0:T(2,128)(2,1)} %param.8, f32[]{:T(128)S(6)} %div.20), kind=kLoop, calls=%fused_computation.49 | loop fusion | flops 16383 | bytes 8200 | tf_op jit(solution)/shard_map/reduce_sum | solution.py:44
  16.1 0.6 fusion.60
  17.4 0.6 multiply_reduce_fusion.1
  18.7 0.8 fusion.26
  19.5 14.7 %all-gather = bf16[8,1,4096]{2,1,0:T(2,128)(2,1)S(1)} all-gather(bf16[1,1,4096]{2,1,0:T(2,128)(2,1)S(1)} %get-tuple-element.14), channel_id=1, replica_groups=mesh['section'=2,'mirror'=2,'dp'=8] {'dp'}, dimensions={0}, use_global_device_ids=true | all-gather | bytes 73728 | tf_op jit(solution)/shard_map/all_gather | solution.py:85
  34.2 3.3 %collective-permute-start.2 = (bf16[1,4096]{1,0:T(2,128)(2,1)S(1)}, bf16[1,4096]{1,0:T(2,128)(2,1)S(1)}, u32[]{:S(2)}, u32[]{:S(2)}) collective-permute-start(bf16[1,4096]{1,0:T(2,128)(2,1)S(1)} %fusion.20), channel_id=1, source_target_pairs={{0,7},{1,0},{2,1},{3,2},{4,3},{5,4},{6,5},{7,6},{8,15},{9,8},{10,9... | collective-permute-start | bytes 24584 | tf_op jit(solution)/shard_map/ppermute | solution.py:16
  37.6 2.4 %fusion.2 = f32[8,4096]{1,0:T(8,128)} fusion(bf16[1,128,4096]{2,1,0:T(8,128)(2,1)} %param.11, bf16[1,4096,128]{2,1,0:T(8,128)(2,1)S(1)} %copy-done, bf16[8,1,4096]{2,1,0:T(2,128)(2,1)S(1)} %all-gather), kind=kOutput, calls=%fused_computation.6 | convolution fusion | flops 16786432 | bytes 2293760 | tf_op jit(solution)/shard_map/dot_general | solution.py:98
  40.2 14.1 %all-gather.1 = bf16[8,1,4096]{2,1,0:T(2,128)(2,1)S(1)} all-gather(bf16[1,1,4096]{2,1,0:T(2,128)(2,1)S(1)} %get-tuple-element.13), channel_id=1, replica_groups=mesh['section'=2,'mirror'=2,'dp'=8] {'dp'}, dimensions={0}, use_global_device_ids=true | all-gather | bytes 73728 | tf_op jit(solution)/shard_map/all_gather | solution.py:86
  54.3 0.6 collective-permute-start.4
  55.3 4.3 %collective-permute-done.4 = bf16[4,4096]{1,0:T(4,128)(2,1)S(1)} collective-permute-done((bf16[4,4096]{1,0:T(4,128)(2,1)S(1)}, bf16[4,4096]{1,0:T(4,128)(2,1)S(1)}, u32[]{:S(2)}, u32[]{:S(2)}) %collective-permute-start.4) | collective-permute-done | bytes 32800 | tf_op jit(solution)/shard_map/ppermute | solution.py:16
  60.2 1.0 fusion.4
  61.3 1.5 %convolution_convert_fusion = bf16[4096,128]{1,0:T(8,128)(2,1)} fusion(bf16[8,128]{1,0:T(8,128)(2,1)S(1)} %fusion, bf16[8,1,4096]{2,1,0:T(2,128)(2,1)S(1)} %all-gather.1), kind=kOutput, calls=%fused_computation | convolution fusion | flops 8912896 | bytes 1116160 | tf_op jit(solution)/shard_map/dot_general | solution.py:121
  62.9 0.6 dynamic-slice
  63.5 1.5 %collective-permute-start.5 = (bf16[8,128]{1,0:T(8,128)(2,1)S(1)}, bf16[8,128]{1,0:T(8,128)(2,1)S(1)}, u32[]{:S(2)}, u32[]{:S(2)}) collective-permute-start(bf16[8,128]{1,0:T(8,128)(2,1)S(1)} %get-tuple-element.15), channel_id=1, source_target_pairs={{0,8},{8,0},{1,9},{9,1},{2,10},{10,2},{3,11},{11,3},{4,12},{12,4},... | collective-permute-start | bytes 6152 | tf_op jit(solution)/shard_map/ppermute | solution.py:39
  65.1 0.6 collective-permute-start.6
  66.1 1.0 collective-permute-done.5
  67.1 2.0 %collective-permute-done.6 = bf16[8,2048]{1,0:T(8,128)(2,1)S(1)} collective-permute-done((bf16[8,2048]{1,0:T(8,128)(2,1)S(1)}, bf16[8,2048]{1,0:T(8,128)(2,1)S(1)}, u32[]{:S(2)}, u32[]{:S(2)}) %collective-permute-start.6) | collective-permute-done | bytes 32800 | tf_op jit(solution)/shard_map/ppermute | solution.py:39
  69.5 0.9 fusion.10
  70.4 45.9 %all-reduce.5.cloned.1.call-done = (f32[8,4096]{1,0:T(8,128)}, f32[8,4096]{1,0:T(8,128)}) async-done(((f32[8,4096]{1,0:T(8,128)}, f32[8,4096]{1,0:T(8,128)}), (f32[8,4096]{1,0:T(8,128)}, f32[8,4096]{1,0:T(8,128)})) %all-reduce.5.cloned.1.call-update) | async-done | bytes 262160
  116.3 2.2 %fusion.59 = (f32[]{:T(128)}, f32[]{:T(128)}, f32[1,4096]{1,0:T(1,128)S(1)}) fusion(f32[]{:T(128)S(6)} %rsqrt.9, f32[]{:T(128)S(6)} %div.20, bf16[1,1,1,4096]{3,2,1,0:T(2,128)(2,1)S(1)} %copy-done.2, f32[1,4096]{1,0:T(1,128)S(1)} %copy-done.3, f32[8,4096]{1,0:T(8,128)} %get-tuple-element.7, u32[]{:T(128)} %bitcast.13), kind=kLoop, calls=%fused_computation.78 | loop fusion | flops 28670 | bytes 57364 | tf_op jit(solution)/shard_map/reduce_sum | solution.py:114
  119.8 2.2 %fusion.24 = (bf16[1,1,1,4096]{3,2,1,0:T(2,128)(2,1)}, bf16[1,1,1,4096]{3,2,1,0:T(2,128)(2,1)}) fusion(f32[8,4096]{1,0:T(8,128)} %get-tuple-element.6, u32[]{:T(128)} %bitcast.13, f32[1,1,4096]{2,1,0:T(1,128)S(1)} %get-tuple-element.10, f32[]{:T(128)S(6)} %div.23, f32[]{:T(128)S(6)} %rsqrt.9, f32[]{:T(128)S(6)} %div.20, ...), kind=kLoop, calls=%fused_computation.37 | loop fusion | flops 49152 | bytes 84484 | tf_op jit(solution)/shard_map/broadcast_in_dim | solution.py:135
  (30 shorter events, 2.1 us)
Async XLA Ops:
  8.0 29.6 %copy-start = (bf16[1,4096,128]{2,1,0:T(8,128)(2,1)S(1)}, bf16[1,4096,128]{2,1,0:T(8,128)(2,1)}, u32[]{:S(2)}) copy-start(bf16[1,4096,128]{2,1,0:T(8,128)(2,1)} %param.10) | copy-start | bytes 3145732
  8.0 108.2 %all-reduce.5.cloned.1.call-start = ((), (), s32[]{:S(2)}) async-start(), calls=%async_computation.2 | async-start | bytes 524288
  8.9 7.2 %collective-permute-start = (bf16[1,1,4096]{2,1,0:T(2,128)(2,1)S(1)}, bf16[1,1,4096]{2,1,0:T(2,128)(2,1)S(1)}, u32[]{:S(2)}, u32[]{:S(2)}) collective-permute-start(bf16[1,1,4096]{2,1,0:T(2,128)(2,1)S(1)} %get-tuple-element.12), channel_id=1, source_target_pairs={{0,16},{16,0},{1,17},{17,1},{2,18},{18,2},{3,19},{19,3},{4,20},{20... | collective-permute-start | bytes 24584 | tf_op jit(solution)/shard_map/ppermute | solution.py:28
  11.9 4.2 %collective-permute-start.1 = (bf16[1,1,4096]{2,1,0:T(2,128)(2,1)S(1)}, bf16[1,1,4096]{2,1,0:T(2,128)(2,1)S(1)}, u32[]{:S(2)}, u32[]{:S(2)}) collective-permute-start(bf16[1,1,4096]{2,1,0:T(2,128)(2,1)S(1)} %get-tuple-element.11), channel_id=1, source_target_pairs={{16,0},{0,16},{17,1},{1,17},{18,2},{2,18},{19,3},{3,19},{20,4},{4,... | collective-permute-start | bytes 24584 | tf_op jit(solution)/shard_map/ppermute | solution.py:31
  34.2 5.7 %collective-permute-start.2 = (bf16[1,4096]{1,0:T(2,128)(2,1)S(1)}, bf16[1,4096]{1,0:T(2,128)(2,1)S(1)}, u32[]{:S(2)}, u32[]{:S(2)}) collective-permute-start(bf16[1,4096]{1,0:T(2,128)(2,1)S(1)} %fusion.20), channel_id=1, source_target_pairs={{0,7},{1,0},{2,1},{3,2},{4,3},{5,4},{6,5},{7,6},{8,15},{9,8},{10,9... | collective-permute-start | bytes 24584 | tf_op jit(solution)/shard_map/ppermute | solution.py:16
  40.0 19.8 %copy-start.1 = (bf16[1,128,4096]{2,1,0:T(8,128)(2,1)S(1)}, bf16[1,128,4096]{2,1,0:T(8,128)(2,1)}, u32[]{:S(2)}) copy-start(bf16[1,128,4096]{2,1,0:T(8,128)(2,1)} %param.11) | copy-start | bytes 3145732
  40.0 14.2 %collective-permute-start.3 = (bf16[2,4096]{1,0:T(2,128)(2,1)S(1)}, bf16[2,4096]{1,0:T(2,128)(2,1)S(1)}, u32[]{:S(2)}, u32[]{:S(2)}) collective-permute-start(bf16[2,4096]{1,0:T(2,128)(2,1)S(1)} %pad_maximum_fusion.1), channel_id=1, source_target_pairs={{0,6},{1,7},{2,0},{3,1},{4,2},{5,3},{6,4},{7,5},{8,14},{9,15},{10,... | collective-permute-start | bytes 49160 | tf_op jit(solution)/shard_map/ppermute | solution.py:16
  54.3 5.3 %collective-permute-start.4 = (bf16[4,4096]{1,0:T(4,128)(2,1)S(1)}, bf16[4,4096]{1,0:T(4,128)(2,1)S(1)}, u32[]{:S(2)}, u32[]{:S(2)}) collective-permute-start(bf16[4,4096]{1,0:T(4,128)(2,1)S(1)} %pad_maximum_fusion), channel_id=1, source_target_pairs={{0,4},{1,5},{2,6},{3,7},{4,0},{5,1},{6,2},{7,3},{8,12},{9,13},{10,... | collective-permute-start | bytes 98312 | tf_op jit(solution)/shard_map/ppermute | solution.py:16
  61.3 1.6 %copy-start.4 = (u32[32]{0:T(128)S(1)}, u32[32]{0:T(128)}, u32[]{:S(2)}) copy-start(u32[32]{0:T(128)} %constant.96) | copy-start | bytes 388
  61.3 60.7 %reduce-scatter.2.cloned.1.call-start = ((), (), s32[]{:S(2)}) async-start(), calls=%async_computation.1 | async-start | bytes 1572864 | tf_op jit(solution)/shard_map/reduce_scatter | solution.py:122
  63.5 3.6 %collective-permute-start.5 = (bf16[8,128]{1,0:T(8,128)(2,1)S(1)}, bf16[8,128]{1,0:T(8,128)(2,1)S(1)}, u32[]{:S(2)}, u32[]{:S(2)}) collective-permute-start(bf16[8,128]{1,0:T(8,128)(2,1)S(1)} %get-tuple-element.15), channel_id=1, source_target_pairs={{0,8},{8,0},{1,9},{9,1},{2,10},{10,2},{3,11},{11,3},{4,12},{12,4},... | collective-permute-start | bytes 6152 | tf_op jit(solution)/shard_map/ppermute | solution.py:39
  65.1 4.0 %collective-permute-start.6 = (bf16[8,2048]{1,0:T(8,128)(2,1)S(1)}, bf16[8,2048]{1,0:T(8,128)(2,1)S(1)}, u32[]{:S(2)}, u32[]{:S(2)}) collective-permute-start(bf16[8,2048]{1,0:T(8,128)(2,1)S(1)} %dynamic_slice.12), channel_id=1, source_target_pairs={{0,8},{8,0},{1,9},{9,1},{2,10},{10,2},{3,11},{11,3},{4,12},{12,4},... | collective-permute-start | bytes 98312 | tf_op jit(solution)/shard_map/ppermute | solution.py:39
  66.1 50.2 %copy-start.2 = (bf16[1,1,1,4096]{3,2,1,0:T(2,128)(2,1)S(1)}, bf16[1,1,1,4096]{3,2,1,0:T(2,128)(2,1)}, u32[]{:S(2)}) copy-start(bf16[1,1,1,4096]{3,2,1,0:T(2,128)(2,1)} %param.8) | copy-start | bytes 24580
  66.1 50.2 %copy-start.3 = (f32[1,4096]{1,0:T(1,128)S(1)}, f32[1,4096]{1,0:T(1,128)}, u32[]{:S(2)}) copy-start(f32[1,4096]{1,0:T(1,128)} %param.9) | copy-start | bytes 49156
Sparse Core Ops, SparseCore 0:
  61.4 54.8 all-reduce.4
Sparse Core Ops, SparseCore 1:
  64.7 19.9 reduce-scatter.1
